TPU v7x, 32 devices: a whole 2x2x4 slice. The times are simulated.
32 devices in a mesh: member: 2 (over y), lon: 4 (over z), lat: 2 (over x), dp: 2 (over core).
Axes of the slice: x: 2, y: 2, z: 4, core: 2. Of those that a mesh axis runs over, the one named last changes fastest.
Arguments:
- fields: bfloat16 [4, 64, 32, 512], P(('member', 'dp'), 'lat', 'lon'), parts along dimension 0, may hold values from -6 to 6
- cotangent: bfloat16 [4, 64, 32, 512], P(('member', 'dp'), 'lat', 'lon'), parts along dimension 0, may hold values from -6 to 6
- conv_weight: float32 [7, 7, 512], replicated, may hold values from -0.875 to 0.875
- norm_gain: float32 [512], replicated, may hold values from 0.1 to 1.9
- w_qkv: bfloat16 [512, 768], replicated, may hold values from -1 to 1
- w_out: bfloat16 [256, 512], replicated, may hold values from -0.375 to 0.375
Outputs:
- result: bfloat16 [4, 64, 32, 512], P(('member', 'dp'), 'lat', 'lon'), parts along dimension 0
- grad_fields: bfloat16 [4, 64, 32, 512], P(('member', 'dp'), 'lat', 'lon'), parts along dimension 0
- grad_qkv: float32 [1024, 768], P('member'), parts along dimension 0
- grad_out: float32 [512, 512], P('member'), parts along dimension 0
- grad_conv: float32 [14, 7, 512], P('member'), parts along dimension 0
- grad_gain: float32 [1024], P('member'), parts along dimension 0
There are 2 independent parts, one for each index of `member`. A program takes and returns all parts, laid end to end along the dimension named above; an argument that names none is the same for every part. Nothing has to cross between parts.
All inputs are finite; a program needn't handle non-finite values.
Results may differ from a plain program's by a relative error of at most 0.012.
The roundings to bfloat16 on the way count: a program that leaves them out, or rounds other values in their place, can miss the bound.
Values may be sent and summed in bfloat16 or wider, within the bound.
A program may use at most 64 MiB of HBM per device.

v0:
```python
import jax
import jax.numpy as jnp
from jax import lax
from jax.sharding import PartitionSpec as P

HEADS = 4
HEAD_DIM = 64
EPSILON = 1e-06


def with_halo(x, sides, width, wrap):
    for axis, dim in sides:
        size, length = (lax.axis_size(axis), x.shape[dim])
        up = [(i, (i + 1) % size) for i in range(size if wrap else size - 1)]
        down = [(j, i) for i, j in up]
        last = lax.slice_in_dim(x, length - width, length, axis=dim)
        first = lax.slice_in_dim(x, 0, width, axis=dim)
        before = lax.ppermute(last, axis, up)
        after = lax.ppermute(first, axis, down)
        x = jnp.concatenate([before, x, after], axis=dim)
    return x


def spread(padded, kernel, lat_rows, lon_cols):
    summed = jnp.zeros(padded.shape[:1] + (lat_rows, lon_cols, padded.shape[3]), jnp.float32)
    for row_shift in range(7):
        band = padded[:, row_shift : row_shift + lat_rows].astype(jnp.float32)
        partial_row = kernel[row_shift, 0] * band[:, :, 0:lon_cols]
        for col_shift in range(1, 7):
            partial_row = (
                partial_row
                + kernel[row_shift, col_shift] * band[:, :, col_shift : col_shift + lon_cols]
            )
        summed = summed + partial_row
    return summed


def correlate(padded, upstream, lat_rows, lon_cols):
    pieces = []
    for row_shift in range(7):
        for col_shift in range(7):
            window = padded[
                :, row_shift : row_shift + lat_rows, col_shift : col_shift + lon_cols
            ].astype(jnp.float32)
            pieces.append(jnp.sum(window * upstream, axis=(0, 1, 2)))
    return jnp.stack(pieces).reshape(7, 7, -1)


def split_heads(values):
    return values.reshape(values.shape[:-1] + (HEADS, HEAD_DIM))


def attend_forward(rowwise, att_width):
    queries = split_heads(rowwise[..., :att_width])
    keys_part = split_heads(rowwise[..., att_width : 2 * att_width])
    values_part = split_heads(rowwise[..., 2 * att_width :])
    scores = jnp.einsum(
        "brqhd,brkhd->brhqk", queries, keys_part, preferred_element_type=jnp.float32
    ) * HEAD_DIM ** (-0.5)
    row_peak = jnp.max(scores, -1, keepdims=True)
    raised = jnp.exp(scores - row_peak)
    probs = raised / jnp.sum(raised, -1, keepdims=True)
    weights = probs.astype(jnp.bfloat16)
    mixed = jnp.einsum(
        "brhqk,brkhd->brqhd", weights, values_part, preferred_element_type=jnp.float32
    )
    return (mixed.reshape(rowwise.shape[:3] + (att_width,)).astype(jnp.bfloat16), probs)


def attend_backward(rowwise, probs, grad_rowwise, att_width):
    queries = split_heads(rowwise[..., :att_width])
    keys_part = split_heads(rowwise[..., att_width : 2 * att_width])
    values_part = split_heads(rowwise[..., 2 * att_width :])
    grad_heads = split_heads(grad_rowwise)
    weights = probs.astype(jnp.bfloat16)
    grad_probs = jnp.einsum(
        "brqhd,brkhd->brhqk", grad_heads, values_part, preferred_element_type=jnp.float32
    )
    inner = jnp.sum(probs * grad_probs, -1, keepdims=True)
    grad_scores = (probs * (grad_probs - inner) * HEAD_DIM ** (-0.5)).astype(jnp.bfloat16)
    grad_query = jnp.einsum(
        "brhqk,brkhd->brqhd", grad_scores, keys_part, preferred_element_type=jnp.float32
    )
    grad_key = jnp.einsum(
        "brhqk,brqhd->brkhd", grad_scores, queries, preferred_element_type=jnp.float32
    )
    grad_value = jnp.einsum(
        "brhqk,brqhd->brkhd", weights, grad_heads, preferred_element_type=jnp.float32
    )
    shaped = rowwise.shape[:3] + (att_width,)
    return jnp.concatenate(
        [
            grad_query.reshape(shaped).astype(jnp.bfloat16),
            grad_key.reshape(shaped).astype(jnp.bfloat16),
            grad_value.reshape(shaped).astype(jnp.bfloat16),
        ],
        axis=-1,
    )


def contract_rows(left, right):
    return lax.dot_general(
        left, right, (((0,), (0,)), ((), ())), preferred_element_type=jnp.float32
    )


def contract_cols(left, right):
    return lax.dot_general(
        left, right, (((1,), (1,)), ((), ())), preferred_element_type=jnp.float32
    )


def on_device(fields, cotangent, conv_weight, norm_gain, w_qkv, w_out):
    batch_count, lat_rows, lon_cols, channels = fields.shape
    att_width = w_out.shape[0]
    wide = with_halo(fields, (("lon", 2),), 3, True)
    padded = with_halo(wide, (("lat", 1),), 3, False)
    update = fields.astype(jnp.float32) + spread(padded, conv_weight, lat_rows, lon_cols)
    inverse = lax.rsqrt(jnp.mean(update * update, -1, keepdims=True) + EPSILON)
    normed = (update * inverse * norm_gain).astype(jnp.bfloat16)
    normed_flat = normed.reshape(-1, channels)
    projected = jnp.dot(normed_flat, w_qkv, preferred_element_type=jnp.float32).astype(jnp.bfloat16)
    rowwise = lax.all_to_all(
        projected.reshape(batch_count, lat_rows, lon_cols, 3 * att_width),
        "lon",
        split_axis=1,
        concat_axis=2,
        tiled=True,
    )
    mixed_rows, probs = attend_forward(rowwise, att_width)
    mixed = lax.all_to_all(mixed_rows, "lon", split_axis=2, concat_axis=1, tiled=True)
    mixed_flat = mixed.reshape(-1, att_width)
    result = (
        update
        + jnp.dot(mixed_flat, w_out, preferred_element_type=jnp.float32).reshape(update.shape)
    ).astype(jnp.bfloat16)
    upstream_flat = cotangent.reshape(-1, channels)
    grad_mixed = contract_cols(upstream_flat, w_out).astype(jnp.bfloat16)
    grad_out = contract_rows(mixed_flat, upstream_flat)
    grad_rowwise = lax.all_to_all(
        grad_mixed.reshape(batch_count, lat_rows, lon_cols, att_width),
        "lon",
        split_axis=1,
        concat_axis=2,
        tiled=True,
    )
    grad_projected_rows = attend_backward(rowwise, probs, grad_rowwise, att_width)
    grad_projected = lax.all_to_all(
        grad_projected_rows, "lon", split_axis=2, concat_axis=1, tiled=True
    )
    grad_flat = grad_projected.reshape(-1, 3 * att_width)
    grad_weight = contract_rows(normed_flat, grad_flat)
    grad_normed = contract_cols(grad_flat, w_qkv).reshape(update.shape)
    grad_gain = jnp.sum(grad_normed * (update * inverse), axis=(0, 1, 2))
    gained = norm_gain * grad_normed
    grad_update = (
        cotangent.astype(jnp.float32)
        + inverse * gained
        - update * inverse**3 * jnp.mean(gained * update, -1, keepdims=True)
    )
    grad_wide = with_halo(grad_update.astype(jnp.bfloat16), (("lon", 2),), 3, True).astype(
        grad_update.dtype
    )
    grad_padded = with_halo(grad_wide.astype(jnp.bfloat16), (("lat", 1),), 3, False).astype(
        grad_wide.dtype
    )
    grad_fields = (
        grad_update + spread(grad_padded, conv_weight[::-1, ::-1], lat_rows, lon_cols)
    ).astype(jnp.bfloat16)
    grad_conv = correlate(padded, grad_update, lat_rows, lon_cols)
    totals = lax.psum((grad_weight, grad_out, grad_conv, grad_gain), ("lon", "lat", "dp"))
    return (result, grad_fields, totals[0], totals[1], totals[2], totals[3])


def solution(mesh):
    placed = (
        P(("member", "dp"), "lat", "lon", None),
        P(("member", "dp"), "lat", "lon", None),
        P(),
        P(),
        P(),
        P(),
    )
    return jax.shard_map(
        on_device,
        mesh=mesh,
        in_specs=placed,
        out_specs=(
            P(("member", "dp"), "lat", "lon", None),
            P(("member", "dp"), "lat", "lon", None),
            P("member", None),
            P("member", None),
            P("member", None, None),
            P("member"),
        ),
        check_vma=False,
    )
```

profile of v0, /device:TPU:0, one launch (start us, length us, event | category | flops | bytes accessed | tf_op | source)
XLA Modules:
  0.0 233.1 jit_solution(6971295654083758024)
XLA Ops:
  7.2 1.2 fusion.160
  8.4 3.1 %collective-permute-start = (bf16[1,32,3,512]{3,2,1,0:T(4,128)(2,1)S(1)}, bf16[1,32,3,512]{3,2,1,0:T(4,128)(2,1)S(1)}, u32[]{:S(2)}, u32[]{:S(2)}) collective-permute-start(bf16[1,32,3,512]{3,2,1,0:T(4,128)(2,1)S(1)} %get-tuple-element.93), channel_id=1, source_target_pairs={{0,4},{4,8},{8,12},{12,0},{1,5},{5,9},{9,13},{13,1},{2,6},{6,10},{... | collective-permute-start | bytes 294920 | tf_op jit(solution)/shard_map/ppermute | solution.py:18
  11.6 2.1 collective-permute-start.1
  13.6 1.9 fusion.15
  15.6 3.9 %all-to-all-start.2 = ((bf16[1,32,8,256]{3,2,0,1:T(8,128)(2,1)}), bf16[1,32,8,256]{3,2,0,1:T(8,128)(2,1)}, u32[]{:S(2)}, u32[]{:S(2)}) async-start(bf16[1,32,8,256]{3,2,0,1:T(8,128)(2,1)} %fusion.15), calls=%async_computation.2 | async-start | bytes 262144 | tf_op jit(solution)/shard_map/all_to_all | solution.py:140
  19.6 0.6 fusion.161
  20.2 0.7 fusion.162
  20.9 1.2 fusion.156
  22.1 3.5 %collective-permute-start.2 = (bf16[1,3,14,512]{3,2,1,0:T(8,128)(2,1)S(1)}, bf16[1,3,14,512]{3,2,1,0:T(8,128)(2,1)S(1)}, u32[]{:S(2)}, u32[]{:S(2)}) collective-permute-start(bf16[1,3,14,512]{3,2,1,0:T(8,128)(2,1)S(1)} %get-tuple-element.84), channel_id=1, source_target_pairs={{0,2},{1,3},{4,6},{5,7},{8,10},{9,11},{12,14},{13,15},{16,18},{17,... | collective-permute-start | bytes 129032 | tf_op jit(solution)/shard_map/ppermute | solution.py:18
  25.7 1.3 collective-permute-start.3
  27.0 0.6 fusion.163
  27.6 4.0 %collective-permute-done.3 = bf16[1,3,14,512]{3,2,1,0:T(8,128)(2,1)S(1)} collective-permute-done((bf16[1,3,14,512]{3,2,1,0:T(8,128)(2,1)S(1)}, bf16[1,3,14,512]{3,2,1,0:T(8,128)(2,1)S(1)}, u32[]{:S(2)}, u32[]{:S(2)}) %collective-permute-start.3) | collective-permute-done | bytes 43040 | tf_op jit(solution)/shard_map/ppermute | solution.py:19
  31.7 0.3 maximum_maximum_fusion
  32.0 2.0 slice_convert_fusion.2
  34.0 10.5 %multiply_reduce_fusion.51 = (f32[32,8]{1,0:T(8,128)S(1)}, f32[1,32,8,512]{3,2,1,0:T(8,128)S(1)}) fusion(f32[1,32,14,512]{3,2,1,0:T(8,128)S(1)} %get-tuple-element.77, f32[512]{0:T(512)} %bitcast.283, f32[512]{0:T(512)} %bitcast.285, f32[512]{0:T(512)S(1)} %bitcast.191, f32[512]{0:T(512)S(1)} %bitcast.193, f32[512]{0:T(512)S(1)} %bitcast.195, ...), kind=kLoop, calls=%fused_computation.293 | loop fusion | flops 13238016 | bytes 26577920 | tf_op jit(solution)/shard_map/reduce_sum | solution.py:119
  44.6 1.2 fusion.10
  45.7 5.0 %all-to-all-start = ((bf16[1,32,8,768]{3,2,0,1:T(8,128)(2,1)}), bf16[1,32,8,768]{3,2,0,1:T(8,128)(2,1)S(1)}, u32[]{:S(2)}, u32[]{:S(2)}) async-start(bf16[1,32,8,768]{3,2,0,1:T(8,128)(2,1)} %fusion.10), calls=%async_computation | async-start | bytes 786432 | tf_op jit(solution)/shard_map/all_to_all | solution.py:123
  50.8 0.7 constant_dynamic-update-slice_fusion.1
  51.5 1.6 copy.83
  53.1 1.1 reshape.613
  54.2 6.2 %all-to-all-done = bf16[1,32,8,768]{3,2,0,1:T(8,128)(2,1)S(1)} async-done(((bf16[1,32,8,768]{3,2,0,1:T(8,128)(2,1)}), bf16[1,32,8,768]{3,2,0,1:T(8,128)(2,1)S(1)}, u32[]{:S(2)}, u32[]{:S(2)}) %all-to-all-start) | async-done | bytes 393248 | tf_op jit(solution)/shard_map/all_to_all | solution.py:123
  60.4 0.9 reshape.608
  61.3 0.9 reshape.609
  62.3 2.1 fusion.164
  64.5 1.1 fusion.129
  65.5 2.0 fusion.14
  67.5 1.0 fusion.11
  68.6 2.6 %fusion.12 = bf16[1,8,32,4,64]{4,2,3,1,0:T(8,128)(2,1)} fusion(f32[8,4,32,32]{2,3,1,0:T(8,128)} %fusion.129, bf16[8,32,4,64]{3,2,1,0:T(4,128)(2,1)S(1)} %copy-done.18, f32[8,4,32,32]{2,3,1,0:T(8,128)} %get-tuple-element.147, f32[8,4,32]{2,1,0:T(4,128)S(1)} %get-tuple-element.146), kind=kOutput, calls=%fused_computation.20 | convolution fusion | flops 4490271 | bytes 528384 | tf_op jit(solution)/shard_map/brhqk,brkhd->brqhd/dot_general | solution.py:81
  71.2 1.1 copy.88
  72.3 0.9 convert_element_type.322
  73.2 1.1 copy.99
  74.3 0.9 reshape.619
  75.1 3.9 %all-to-all-start.1 = ((bf16[1,8,32,256]{3,1,0,2:T(8,128)(2,1)}), bf16[1,8,32,256]{3,1,0,2:T(8,128)(2,1)}, u32[]{:S(2)}, u32[]{:S(2)}) async-start(bf16[1,8,32,256]{3,1,0,2:T(8,128)(2,1)} %reshape.619), calls=%async_computation.1 | async-start | bytes 262144 | tf_op jit(solution)/shard_map/all_to_all | solution.py:131
  79.1 2.6 %fusion.13 = bf16[1,8,32,4,64]{4,2,3,1,0:T(8,128)(2,1)} fusion(f32[8,4,32,32]{2,3,1,0:T(8,128)} %fusion.129, bf16[8,32,4,64]{3,2,1,0:T(4,128)(2,1)S(1)} %copy-done.17, f32[8,4,32,32]{2,3,1,0:T(8,128)} %get-tuple-element.147, f32[8,4,32]{2,1,0:T(4,128)S(1)} %get-tuple-element.146), kind=kOutput, calls=%fused_computation.21 | convolution fusion | flops 4490271 | bytes 528384 | tf_op jit(solution)/shard_map/brhqk,brqhd->brkhd/dot_general | solution.py:84
  81.7 1.1 copy.90
  82.8 0.9 convert_element_type.326
  83.6 1.1 copy.92
  84.7 0.9 convert_element_type.330
  85.6 1.1 pad_maximum_fusion.2
  86.7 1.0 copy.93
  87.6 5.0 %all-to-all-start.3 = ((bf16[1,8,32,768]{3,1,0,2:T(8,128)(2,1)}), bf16[1,8,32,768]{3,1,0,2:T(8,128)(2,1)S(1)}, u32[]{:S(2)}, u32[]{:S(2)}) async-start(bf16[1,8,32,768]{3,1,0,2:T(8,128)(2,1)} %copy.93), calls=%async_computation.3 | async-start | bytes 786432 | tf_op jit(solution)/shard_map/all_to_all | solution.py:148
  92.7 1.7 constant_dynamic-update-slice_fusion
  94.3 0.9 copy.134
  95.3 1.0 fusion.122
  96.3 0.9 fusion.9
  97.3 4.3 %all-to-all-done.3 = bf16[1,8,32,768]{3,1,0,2:T(8,128)(2,1)S(1)} async-done(((bf16[1,8,32,768]{3,1,0,2:T(8,128)(2,1)}), bf16[1,8,32,768]{3,1,0,2:T(8,128)(2,1)S(1)}, u32[]{:S(2)}, u32[]{:S(2)}) %all-to-all-start.3) | async-done | bytes 393248 | tf_op jit(solution)/shard_map/all_to_all | solution.py:148
  101.7 1.0 multiply_reduce_fusion.1
  102.7 2.2 multiply_reduce_fusion.2
  104.9 2.0 multiply_reduce_fusion.29
  107.0 0.6 collective-permute-start.4
  107.6 3.3 %collective-permute-start.5 = (bf16[1,32,3,512]{3,2,1,0:T(4,128)(2,1)S(1)}, bf16[1,32,3,512]{3,2,1,0:T(4,128)(2,1)S(1)}, u32[]{:S(2)}, u32[]{:S(2)}) collective-permute-start(bf16[1,32,3,512]{3,2,1,0:T(4,128)(2,1)S(1)} %get-tuple-element.92), channel_id=1, source_target_pairs={{4,0},{8,4},{12,8},{0,12},{5,1},{9,5},{13,9},{1,13},{6,2},{10,6},{... | collective-permute-start | bytes 294920 | tf_op jit(solution)/shard_map/ppermute | solution.py:19
  110.9 1.7 multiply_reduce_fusion.20
  112.6 1.4 collective-permute-done.4
  114.1 1.9 collective-permute-start.6
  116.3 1.3 collective-permute-start.7
  117.6 1.6 fusion.139
  119.9 0.7 reshape.617
  120.9 0.3 copy-done.93
  121.2 31.5 %psum.31 = f32[512]{0:T(512)} all-reduce(f32[512]{0:T(512)S(1)} %copy-done.93), channel_id=1, replica_groups=mesh['member'=2,'lon'=4,'lat'=2,'dp'=2] {'lon','lat','dp'}, use_global_device_ids=true, to_apply=%region_58.0 | all-reduce | flops 512 | bytes 4096 | tf_op jit(solution)/shard_map/psum | solution.py:171
  153.3 4.5 %fusion.24 = bf16[1,32,8,512]{3,2,1,0:T(8,128)(2,1)} fusion(f32[1,32,8,512]{3,2,1,0:T(8,128)S(1)} %get-tuple-element.70, f32[1,38,14,512]{3,2,1,0:T(8,128)S(1)} %maximum_convert_fusion, f32[512]{0:T(512)S(1)} %bitcast.284, f32[512]{0:T(512)S(1)} %bitcast.286, f32[512]{0:T(512)S(1)} %bitcast.192, f32[512]{0:T(512)S(1)} %bitcast.194, f32[512]{0:T(512)S(1)} %bitcast.196, ...), kind=kLoop, calls=%fused_computation.42 | loop fusion | flops 12976128 | bytes 26576896 | tf_op jit(solution)/shard_map/convert_element_type | solution.py:169
  157.8 64.3 %all-reduce.3.cloned.1.call-done = (f32[512,768]{1,0:T(8,128)}, f32[256,512]{1,0:T(8,128)}, f32[7,7,512]{2,1,0:T(8,128)}) async-done(((f32[512,768]{1,0:T(8,128)}, f32[256,512]{1,0:T(8,128)}, f32[7,7,512]{2,1,0:T(8,128)}), (f32[512,768]{1,0:T(8,128)}, f32[256,512]{1,0:T(8,128)}, f32[7,7,512]{2,1,0:T(8,128)})) %all-reduce.3.cloned.1.call-update) | async-done | bytes 2197520 | tf_op jit(solution)/shard_map/psum | solution.py:171
  222.1 2.7 %copy.139 = f32[512,768]{1,0:T(8,128)} copy(f32[512,768]{1,0:T(8,128)} %get-tuple-element.154) | data formatting | bytes 3145728
  224.8 0.8 copy.140
  225.6 0.6 copy.141
  (212 shorter events, 1.5 us)
Async XLA Ops:
  7.2 37.4 %copy-start = (bf16[512,768]{1,0:T(8,128)(2,1)S(1)}, bf16[512,768]{1,0:T(8,128)(2,1)}, u32[]{:S(2)}) copy-start(bf16[512,768]{1,0:T(8,128)(2,1)} %param.10) | copy-start | bytes 2359300
  7.2 13.7 %copy-start.1 = (bf16[1,32,8,512]{3,2,1,0:T(8,128)(2,1)S(1)}, bf16[1,32,8,512]{3,2,1,0:T(8,128)(2,1)}, u32[]{:S(2)}) copy-start(bf16[1,32,8,512]{3,2,1,0:T(8,128)(2,1)} %param.6) | copy-start | bytes 786436
  7.2 12.3 %copy-start.20 = (f32[7,7,512]{2,1,0:T(8,128)S(1)}, f32[7,7,512]{2,1,0:T(8,128)}, u32[]{:S(2)}) copy-start(f32[7,7,512]{2,1,0:T(8,128)} %param.8) | copy-start | bytes 301060
  8.4 12.4 %collective-permute-start = (bf16[1,32,3,512]{3,2,1,0:T(4,128)(2,1)S(1)}, bf16[1,32,3,512]{3,2,1,0:T(4,128)(2,1)S(1)}, u32[]{:S(2)}, u32[]{:S(2)}) collective-permute-start(bf16[1,32,3,512]{3,2,1,0:T(4,128)(2,1)S(1)} %get-tuple-element.93), channel_id=1, source_target_pairs={{0,4},{4,8},{8,12},{12,0},{1,5},{5,9},{9,13},{13,1},{2,6},{6,10},{... | collective-permute-start | bytes 294920 | tf_op jit(solution)/shard_map/ppermute | solution.py:18
  11.6 9.3 %collective-permute-start.1 = (bf16[1,32,3,512]{3,2,1,0:T(4,128)(2,1)S(1)}, bf16[1,32,3,512]{3,2,1,0:T(4,128)(2,1)S(1)}, u32[]{:S(2)}, u32[]{:S(2)}) collective-permute-start(bf16[1,32,3,512]{3,2,1,0:T(4,128)(2,1)S(1)} %get-tuple-element.94), channel_id=1, source_target_pairs={{4,0},{8,4},{12,8},{0,12},{5,1},{9,5},{13,9},{1,13},{6,2},{10,6},{... | collective-permute-start | bytes 294920 | tf_op jit(solution)/shard_map/ppermute | solution.py:19
  15.6 30.2 %all-to-all-start.2 = ((bf16[1,32,8,256]{3,2,0,1:T(8,128)(2,1)}), bf16[1,32,8,256]{3,2,0,1:T(8,128)(2,1)}, u32[]{:S(2)}, u32[]{:S(2)}) async-start(bf16[1,32,8,256]{3,2,0,1:T(8,128)(2,1)} %fusion.15), calls=%async_computation.2 | async-start | bytes 262144 | tf_op jit(solution)/shard_map/all_to_all | solution.py:140
  20.8 11.2 %copy-start.8 = (bf16[1,32,3,512]{3,2,1,0:T(4,128)(2,1)}, bf16[1,32,3,512]{3,2,1,0:T(4,128)(2,1)S(1)}, u32[]{:S(2)}) copy-start(bf16[1,32,3,512]{3,2,1,0:T(4,128)(2,1)S(1)} %collective-permute-done) | copy-start | bytes 294916
  20.9 11.1 %copy-start.10 = (bf16[1,32,3,512]{3,2,1,0:T(4,128)(2,1)}, bf16[1,32,3,512]{3,2,1,0:T(4,128)(2,1)S(1)}, u32[]{:S(2)}) copy-start(bf16[1,32,3,512]{3,2,1,0:T(4,128)(2,1)S(1)} %collective-permute-done.1) | copy-start | bytes 294916
  22.1 5.5 %collective-permute-start.2 = (bf16[1,3,14,512]{3,2,1,0:T(8,128)(2,1)S(1)}, bf16[1,3,14,512]{3,2,1,0:T(8,128)(2,1)S(1)}, u32[]{:S(2)}, u32[]{:S(2)}) collective-permute-start(bf16[1,3,14,512]{3,2,1,0:T(8,128)(2,1)S(1)} %get-tuple-element.84), channel_id=1, source_target_pairs={{0,2},{1,3},{4,6},{5,7},{8,10},{9,11},{12,14},{13,15},{16,18},{17,... | collective-permute-start | bytes 129032 | tf_op jit(solution)/shard_map/ppermute | solution.py:18
  25.7 6.0 %collective-permute-start.3 = (bf16[1,3,14,512]{3,2,1,0:T(8,128)(2,1)S(1)}, bf16[1,3,14,512]{3,2,1,0:T(8,128)(2,1)S(1)}, u32[]{:S(2)}, u32[]{:S(2)}) collective-permute-start(bf16[1,3,14,512]{3,2,1,0:T(8,128)(2,1)S(1)} %get-tuple-element.85), channel_id=1, source_target_pairs={{2,0},{3,1},{6,4},{7,5},{10,8},{11,9},{14,12},{15,13},{18,16},{19,... | collective-permute-start | bytes 129032 | tf_op jit(solution)/shard_map/ppermute | solution.py:19
  34.0 10.5 %copy-start.21 = (f32[512]{0:T(512)S(1)}, f32[512]{0:T(512)}, u32[]{:S(2)}) copy-start(f32[512]{0:T(512)} %param.9) | copy-start | bytes 6148
  44.5 6.2 %copy-start.2 = (bf16[1,32,8,512]{3,2,1,0:T(8,128)(2,1)S(1)}, bf16[1,32,8,512]{3,2,1,0:T(8,128)(2,1)}, u32[]{:S(2)}) copy-start(bf16[1,32,8,512]{3,2,1,0:T(8,128)(2,1)} %param.6) | copy-start | bytes 786436
  45.7 14.6 %all-to-all-start = ((bf16[1,32,8,768]{3,2,0,1:T(8,128)(2,1)}), bf16[1,32,8,768]{3,2,0,1:T(8,128)(2,1)S(1)}, u32[]{:S(2)}, u32[]{:S(2)}) async-start(bf16[1,32,8,768]{3,2,0,1:T(8,128)(2,1)} %fusion.10), calls=%async_computation | async-start | bytes 786432 | tf_op jit(solution)/shard_map/all_to_all | solution.py:123
  71.2 7.9 %copy-start.17 = (bf16[8,32,4,64]{3,2,1,0:T(4,128)(2,1)S(1)}, bf16[8,32,4,64]{3,2,1,0:T(4,128)(2,1)}, u32[]{:S(2)}) copy-start(bf16[8,32,4,64]{3,2,1,0:T(4,128)(2,1)} %reshape.608) | copy-start | bytes 393220
  75.1 12.5 %all-to-all-start.1 = ((bf16[1,8,32,256]{3,1,0,2:T(8,128)(2,1)}), bf16[1,8,32,256]{3,1,0,2:T(8,128)(2,1)}, u32[]{:S(2)}, u32[]{:S(2)}) async-start(bf16[1,8,32,256]{3,1,0,2:T(8,128)(2,1)} %reshape.619), calls=%async_computation.1 | async-start | bytes 262144 | tf_op jit(solution)/shard_map/all_to_all | solution.py:131
  86.7 8.6 %copy-start.5 = (bf16[1,32,8,512]{3,2,1,0:T(8,128)(2,1)S(1)}, bf16[1,32,8,512]{3,2,1,0:T(8,128)(2,1)}, u32[]{:S(2)}) copy-start(bf16[1,32,8,512]{3,2,1,0:T(8,128)(2,1)} %param.7) | copy-start | bytes 786436
  87.6 13.9 %all-to-all-start.3 = ((bf16[1,8,32,768]{3,1,0,2:T(8,128)(2,1)}), bf16[1,8,32,768]{3,1,0,2:T(8,128)(2,1)S(1)}, u32[]{:S(2)}, u32[]{:S(2)}) async-start(bf16[1,8,32,768]{3,1,0,2:T(8,128)(2,1)} %copy.93), calls=%async_computation.3 | async-start | bytes 786432 | tf_op jit(solution)/shard_map/all_to_all | solution.py:148
  92.7 129.4 %all-reduce.3.cloned.1.call-start = ((), (), s32[]{:S(2)}) async-start(), calls=%async_computation.4 | async-start | bytes 4423680 | tf_op jit(solution)/shard_map/psum | solution.py:171
  104.9 6.0 %copy-start.7 = (bf16[1,32,11,512]{3,2,1,0:T(8,128)(2,1)S(1)}, bf16[1,32,11,512]{3,2,1,0:T(8,128)(2,1)}, u32[]{:S(2)}) copy-start(bf16[1,32,11,512]{3,2,1,0:T(8,128)(2,1)} %constant_dynamic-update-slice_fusion) | copy-start | bytes 1081348
  104.9 6.0 %copy-start.9 = (bf16[1,32,3,512]{3,2,1,0:T(4,128)(2,1)S(1)}, bf16[1,32,3,512]{3,2,1,0:T(4,128)(2,1)}, u32[]{:S(2)}) copy-start(bf16[1,32,3,512]{3,2,1,0:T(4,128)(2,1)} %copy-done.8) | copy-start | bytes 294916
  106.9 7.1 %copy-start.3 = (bf16[1,32,8,512]{3,2,1,0:T(8,128)(2,1)}, bf16[1,32,8,512]{3,2,1,0:T(8,128)(2,1)S(1)}, u32[]{:S(2)}) copy-start(bf16[1,32,8,512]{3,2,1,0:T(8,128)(2,1)S(1)} %get-tuple-element.79) | copy-start | bytes 786436
  107.0 6.9 %collective-permute-start.4 = (bf16[1,32,3,512]{3,2,1,0:T(4,128)(2,1)S(1)}, bf16[1,32,3,512]{3,2,1,0:T(4,128)(2,1)S(1)}, u32[]{:S(2)}, u32[]{:S(2)}) collective-permute-start(bf16[1,32,3,512]{3,2,1,0:T(4,128)(2,1)S(1)} %get-tuple-element.91), channel_id=1, source_target_pairs={{0,4},{4,8},{8,12},{12,0},{1,5},{5,9},{9,13},{13,1},{2,6},{6,10},{... | collective-permute-start | bytes 294920 | tf_op jit(solution)/shard_map/ppermute | solution.py:18
  107.6 6.4 %collective-permute-start.5 = (bf16[1,32,3,512]{3,2,1,0:T(4,128)(2,1)S(1)}, bf16[1,32,3,512]{3,2,1,0:T(4,128)(2,1)S(1)}, u32[]{:S(2)}, u32[]{:S(2)}) collective-permute-start(bf16[1,32,3,512]{3,2,1,0:T(4,128)(2,1)S(1)} %get-tuple-element.92), channel_id=1, source_target_pairs={{4,0},{8,4},{12,8},{0,12},{5,1},{9,5},{13,9},{1,13},{6,2},{10,6},{... | collective-permute-start | bytes 294920 | tf_op jit(solution)/shard_map/ppermute | solution.py:19
  114.1 38.6 %collective-permute-start.6 = (bf16[1,3,14,512]{3,2,1,0:T(8,128)(2,1)S(1)}, bf16[1,3,14,512]{3,2,1,0:T(8,128)(2,1)S(1)}, u32[]{:S(2)}, u32[]{:S(2)}) collective-permute-start(bf16[1,3,14,512]{3,2,1,0:T(8,128)(2,1)S(1)} %get-tuple-element.80), channel_id=1, source_target_pairs={{0,2},{1,3},{4,6},{5,7},{8,10},{9,11},{12,14},{13,15},{16,18},{17,... | collective-permute-start | bytes 129032 | tf_op jit(solution)/shard_map/ppermute | solution.py:18
  116.3 36.4 %collective-permute-start.7 = (bf16[1,3,14,512]{3,2,1,0:T(8,128)(2,1)S(1)}, bf16[1,3,14,512]{3,2,1,0:T(8,128)(2,1)S(1)}, u32[]{:S(2)}, u32[]{:S(2)}) collective-permute-start(bf16[1,3,14,512]{3,2,1,0:T(8,128)(2,1)S(1)} %get-tuple-element.81), channel_id=1, source_target_pairs={{2,0},{3,1},{6,4},{7,5},{10,8},{11,9},{14,12},{15,13},{18,16},{19,... | collective-permute-start | bytes 129032 | tf_op jit(solution)/shard_map/ppermute | solution.py:19
  119.8 32.8 %copy-start.4 = (bf16[1,32,8,512]{3,2,1,0:T(8,128)(2,1)S(1)}, bf16[1,32,8,512]{3,2,1,0:T(8,128)(2,1)}, u32[]{:S(2)}) copy-start(bf16[1,32,8,512]{3,2,1,0:T(8,128)(2,1)} %copy-done.3) | copy-start | bytes 786436
  119.8 32.8 %copy-start.13 = (bf16[1,32,3,512]{3,2,1,0:T(4,128)(2,1)S(1)}, bf16[1,32,3,512]{3,2,1,0:T(4,128)(2,1)}, u32[]{:S(2)}) copy-start(bf16[1,32,3,512]{3,2,1,0:T(4,128)(2,1)} %copy-done.12) | copy-start | bytes 294916
  119.8 32.8 %copy-start.15 = (bf16[1,32,3,512]{3,2,1,0:T(4,128)(2,1)S(1)}, bf16[1,32,3,512]{3,2,1,0:T(4,128)(2,1)}, u32[]{:S(2)}) copy-start(bf16[1,32,3,512]{3,2,1,0:T(4,128)(2,1)} %copy-done.14) | copy-start | bytes 294916
  120.5 32.4 %copy-start.22 = (f32[1,1,512]{2,1,0:T(1,128)S(1)}, f32[1,1,512]{2,1,0:T(1,128)}, u32[]{:S(2)}) copy-start(f32[1,1,512]{2,1,0:T(1,128)} %get-tuple-element.108) | copy-start | bytes 6148
  120.6 32.4 %copy-start.23 = (f32[1,1,512]{2,1,0:T(1,128)S(1)}, f32[1,1,512]{2,1,0:T(1,128)}, u32[]{:S(2)}) copy-start(f32[1,1,512]{2,1,0:T(1,128)} %get-tuple-element.109) | copy-start | bytes 6148
  120.6 32.4 %copy-start.24 = (f32[1,1,512]{2,1,0:T(1,128)S(1)}, f32[1,1,512]{2,1,0:T(1,128)}, u32[]{:S(2)}) copy-start(f32[1,1,512]{2,1,0:T(1,128)} %get-tuple-element.110) | copy-start | bytes 6148
  120.6 32.4 %copy-start.25 = (f32[1,1,512]{2,1,0:T(1,128)S(1)}, f32[1,1,512]{2,1,0:T(1,128)}, u32[]{:S(2)}) copy-start(f32[1,1,512]{2,1,0:T(1,128)} %get-tuple-element.111) | copy-start | bytes 6148
  120.6 32.4 %copy-start.26 = (f32[1,1,512]{2,1,0:T(1,128)S(1)}, f32[1,1,512]{2,1,0:T(1,128)}, u32[]{:S(2)}) copy-start(f32[1,1,512]{2,1,0:T(1,128)} %get-tuple-element.112) | copy-start | bytes 6148
  120.6 32.4 %copy-start.27 = (f32[1,1,512]{2,1,0:T(1,128)S(1)}, f32[1,1,512]{2,1,0:T(1,128)}, u32[]{:S(2)}) copy-start(f32[1,1,512]{2,1,0:T(1,128)} %get-tuple-element.113) | copy-start | bytes 6148
  120.6 32.4 %copy-start.28 = (f32[1,1,512]{2,1,0:T(1,128)S(1)}, f32[1,1,512]{2,1,0:T(1,128)}, u32[]{:S(2)}) copy-start(f32[1,1,512]{2,1,0:T(1,128)} %get-tuple-element.114) | copy-start | bytes 6148
  120.6 32.4 %copy-start.29 = (f32[1,1,512]{2,1,0:T(1,128)S(1)}, f32[1,1,512]{2,1,0:T(1,128)}, u32[]{:S(2)}) copy-start(f32[1,1,512]{2,1,0:T(1,128)} %get-tuple-element.115) | copy-start | bytes 6148
  120.6 32.4 %copy-start.30 = (f32[1,1,512]{2,1,0:T(1,128)S(1)}, f32[1,1,512]{2,1,0:T(1,128)}, u32[]{:S(2)}) copy-start(f32[1,1,512]{2,1,0:T(1,128)} %get-tuple-element.116) | copy-start | bytes 6148
  120.6 32.4 %copy-start.31 = (f32[1,1,512]{2,1,0:T(1,128)S(1)}, f32[1,1,512]{2,1,0:T(1,128)}, u32[]{:S(2)}) copy-start(f32[1,1,512]{2,1,0:T(1,128)} %get-tuple-element.117) | copy-start | bytes 6148
  120.6 32.4 %copy-start.32 = (f32[1,1,512]{2,1,0:T(1,128)S(1)}, f32[1,1,512]{2,1,0:T(1,128)}, u32[]{:S(2)}) copy-start(f32[1,1,512]{2,1,0:T(1,128)} %get-tuple-element.118) | copy-start | bytes 6148
  120.7 32.4 %copy-start.33 = (f32[1,1,512]{2,1,0:T(1,128)S(1)}, f32[1,1,512]{2,1,0:T(1,128)}, u32[]{:S(2)}) copy-start(f32[1,1,512]{2,1,0:T(1,128)} %get-tuple-element.119) | copy-start | bytes 6148
  120.7 32.4 %copy-start.34 = (f32[1,1,512]{2,1,0:T(1,128)S(1)}, f32[1,1,512]{2,1,0:T(1,128)}, u32[]{:S(2)}) copy-start(f32[1,1,512]{2,1,0:T(1,128)} %get-tuple-element.120) | copy-start | bytes 6148
  120.7 32.4 %copy-start.35 = (f32[1,1,512]{2,1,0:T(1,128)S(1)}, f32[1,1,512]{2,1,0:T(1,128)}, u32[]{:S(2)}) copy-start(f32[1,1,512]{2,1,0:T(1,128)} %get-tuple-element.121) | copy-start | bytes 6148
  120.7 32.4 %copy-start.36 = (f32[1,1,512]{2,1,0:T(1,128)S(1)}, f32[1,1,512]{2,1,0:T(1,128)}, u32[]{:S(2)}) copy-start(f32[1,1,512]{2,1,0:T(1,128)} %get-tuple-element.122) | copy-start | bytes 6148
  120.7 32.4 %copy-start.37 = (f32[1,1,512]{2,1,0:T(1,128)S(1)}, f32[1,1,512]{2,1,0:T(1,128)}, u32[]{:S(2)}) copy-start(f32[1,1,512]{2,1,0:T(1,128)} %get-tuple-element.123) | copy-start | bytes 6148
  120.7 32.4 %copy-start.38 = (f32[1,1,512]{2,1,0:T(1,128)S(1)}, f32[1,1,512]{2,1,0:T(1,128)}, u32[]{:S(2)}) copy-start(f32[1,1,512]{2,1,0:T(1,128)} %get-tuple-element.124) | copy-start | bytes 6148
  120.7 32.4 %copy-start.39 = (f32[1,1,512]{2,1,0:T(1,128)S(1)}, f32[1,1,512]{2,1,0:T(1,128)}, u32[]{:S(2)}) copy-start(f32[1,1,512]{2,1,0:T(1,128)} %get-tuple-element.125) | copy-start | bytes 6148
  120.7 32.4 %copy-start.40 = (f32[1,1,512]{2,1,0:T(1,128)S(1)}, f32[1,1,512]{2,1,0:T(1,128)}, u32[]{:S(2)}) copy-start(f32[1,1,512]{2,1,0:T(1,128)} %get-tuple-element.126) | copy-start | bytes 6148
  120.7 32.4 %copy-start.41 = (f32[1,1,512]{2,1,0:T(1,128)S(1)}, f32[1,1,512]{2,1,0:T(1,128)}, u32[]{:S(2)}) copy-start(f32[1,1,512]{2,1,0:T(1,128)} %get-tuple-element.127) | copy-start | bytes 6148
  120.7 32.4 %copy-start.42 = (f32[1,1,512]{2,1,0:T(1,128)S(1)}, f32[1,1,512]{2,1,0:T(1,128)}, u32[]{:S(2)}) copy-start(f32[1,1,512]{2,1,0:T(1,128)} %get-tuple-element.128) | copy-start | bytes 6148
  120.8 32.4 %copy-start.43 = (f32[1,1,512]{2,1,0:T(1,128)S(1)}, f32[1,1,512]{2,1,0:T(1,128)}, u32[]{:S(2)}) copy-start(f32[1,1,512]{2,1,0:T(1,128)} %get-tuple-element.129) | copy-start | bytes 6148
  120.8 32.4 %copy-start.44 = (f32[1,1,512]{2,1,0:T(1,128)S(1)}, f32[1,1,512]{2,1,0:T(1,128)}, u32[]{:S(2)}) copy-start(f32[1,1,512]{2,1,0:T(1,128)} %get-tuple-element.130) | copy-start | bytes 6148
  120.8 32.4 %copy-start.45 = (f32[1,1,512]{2,1,0:T(1,128)S(1)}, f32[1,1,512]{2,1,0:T(1,128)}, u32[]{:S(2)}) copy-start(f32[1,1,512]{2,1,0:T(1,128)} %get-tuple-element.131) | copy-start | bytes 6148
  120.8 32.4 %copy-start.46 = (f32[1,1,512]{2,1,0:T(1,128)S(1)}, f32[1,1,512]{2,1,0:T(1,128)}, u32[]{:S(2)}) copy-start(f32[1,1,512]{2,1,0:T(1,128)} %get-tuple-element.132) | copy-start | bytes 6148
  120.8 32.4 %copy-start.47 = (f32[1,1,512]{2,1,0:T(1,128)S(1)}, f32[1,1,512]{2,1,0:T(1,128)}, u32[]{:S(2)}) copy-start(f32[1,1,512]{2,1,0:T(1,128)} %get-tuple-element.133) | copy-start | bytes 6148
  120.8 32.4 %copy-start.48 = (f32[1,1,512]{2,1,0:T(1,128)S(1)}, f32[1,1,512]{2,1,0:T(1,128)}, u32[]{:S(2)}) copy-start(f32[1,1,512]{2,1,0:T(1,128)} %get-tuple-element.134) | copy-start | bytes 6148
  120.8 32.4 %copy-start.49 = (f32[1,1,512]{2,1,0:T(1,128)S(1)}, f32[1,1,512]{2,1,0:T(1,128)}, u32[]{:S(2)}) copy-start(f32[1,1,512]{2,1,0:T(1,128)} %get-tuple-element.135) | copy-start | bytes 6148
  120.8 32.4 %copy-start.50 = (f32[1,1,512]{2,1,0:T(1,128)S(1)}, f32[1,1,512]{2,1,0:T(1,128)}, u32[]{:S(2)}) copy-start(f32[1,1,512]{2,1,0:T(1,128)} %get-tuple-element.136) | copy-start | bytes 6148
  120.8 32.4 %copy-start.51 = (f32[1,1,512]{2,1,0:T(1,128)S(1)}, f32[1,1,512]{2,1,0:T(1,128)}, u32[]{:S(2)}) copy-start(f32[1,1,512]{2,1,0:T(1,128)} %get-tuple-element.137) | copy-start | bytes 6148
  120.8 32.4 %copy-start.52 = (f32[1,1,512]{2,1,0:T(1,128)S(1)}, f32[1,1,512]{2,1,0:T(1,128)}, u32[]{:S(2)}) copy-start(f32[1,1,512]{2,1,0:T(1,128)} %get-tuple-element.138) | copy-start | bytes 6148
  120.9 32.4 %copy-start.53 = (f32[1,1,512]{2,1,0:T(1,128)S(1)}, f32[1,1,512]{2,1,0:T(1,128)}, u32[]{:S(2)}) copy-start(f32[1,1,512]{2,1,0:T(1,128)} %get-tuple-element.139) | copy-start | bytes 6148
  120.9 32.4 %copy-start.54 = (f32[1,1,512]{2,1,0:T(1,128)S(1)}, f32[1,1,512]{2,1,0:T(1,128)}, u32[]{:S(2)}) copy-start(f32[1,1,512]{2,1,0:T(1,128)} %get-tuple-element.140) | copy-start | bytes 6148
  120.9 32.4 %copy-start.55 = (f32[1,1,512]{2,1,0:T(1,128)S(1)}, f32[1,1,512]{2,1,0:T(1,128)}, u32[]{:S(2)}) copy-start(f32[1,1,512]{2,1,0:T(1,128)} %get-tuple-element.141) | copy-start | bytes 6148
  120.9 32.4 %copy-start.56 = (f32[1,1,512]{2,1,0:T(1,128)S(1)}, f32[1,1,512]{2,1,0:T(1,128)}, u32[]{:S(2)}) copy-start(f32[1,1,512]{2,1,0:T(1,128)} %get-tuple-element.142) | copy-start | bytes 6148
  120.9 32.4 %copy-start.57 = (f32[1,1,512]{2,1,0:T(1,128)S(1)}, f32[1,1,512]{2,1,0:T(1,128)}, u32[]{:S(2)}) copy-start(f32[1,1,512]{2,1,0:T(1,128)} %get-tuple-element.143) | copy-start | bytes 6148
  (44 other events, 140.4 us)
Sparse Core Ops, SparseCore 0:
  120.7 101.3 all-reduce.2
where the time goes:
time: 234 us; the launch traced here: 233 us
  waiting for transfers between devices  80.2 us (34%)
  starting transfers between devices  35 us (15%)
  blocking collectives  31.5 us (13%)
  local copies, waits for them, and re-layouts  25.9 us (11%)
  other arithmetic  25.8 us (11%)
  matrix products  19.2 us (8%)
  between operations  15.5 us (7%)
    psum x1, waiting for transfers between devices, on_device(): lax.psum((grad_weight, grad_out, grad_conv, grad_gain), ('lon', 'lat', 'd...  64.3 us
    psum x1, blocking collectives, on_device(): lax.psum((grad_weight, grad_out, grad_conv, grad_gain), ('lon', 'lat', 'd...  31.5 us
    reduce_sum x1, other arithmetic, on_device(): inverse = lax.rsqrt(jnp.mean(update * update, -1, keepdims=True) + EPSILON)  10.5 us
    ppermute x4, starting transfers between devices, with_halo(): before = lax.ppermute(last, axis, up)  9.14 us
    ppermute x4, starting transfers between devices, with_halo(): after = lax.ppermute(first, axis, down)  7.95 us
    all_to_all x1, waiting for transfers between devices, on_device(): lax.all_to_all(projected.reshape(batch_count, lat_rows, lon_cols, 3 * att...  6.17 us
    reduce_sum x3, other arithmetic, correlate(): pieces.append(jnp.sum(window * upstream, axis=(0, 1, 2)))  5.91 us
    unnamed x194, local copies, waits for them, and re-layouts  5.57 us
  transfers between devices with their start and end apart: 13, of which 6 were waited for; matrix products, arithmetic and copies ran while one was open for 19% of the time, Pallas kernels for 0%

commit v1 on v0

--- a/solution.py
+++ b/solution.py
@@ -168,7 +168,10 @@
         grad_update + spread(grad_padded, conv_weight[::-1, ::-1], lat_rows, lon_cols)
     ).astype(jnp.bfloat16)
     grad_conv = correlate(padded, grad_update, lat_rows, lon_cols)
-    totals = lax.psum((grad_weight, grad_out, grad_conv, grad_gain), ("lon", "lat", "dp"))
+    kinds_recover = lambda sample, link_axis, axis_key: lax.psum(
+        lax.psum(sample, link_axis), axis_name=axis_key
+    )
+    totals = kinds_recover((grad_weight, grad_out, grad_conv, grad_gain), "lon", ("lat", "dp"))
     return (result, grad_fields, totals[0], totals[1], totals[2], totals[3])
 
 

time: 234 us -> 270 us (1.15)
  waiting for transfers between devices: 80.2 us -> 129 us
  blocking collectives: 31.5 us -> 20 us
    psum x1 -> x2, waiting for transfers between devices: 64.3 us -> 106 us  [the longest x1 56.9 us: on_device(): lax.psum(sample, link_axis)]
    psum x1 -> x2, blocking collectives: 31.5 us -> 20 us  [the longest x1 13.2 us: on_device(): lax.psum(sample, link_axis)]
    another operation x1, local copies, waits for them, and re-layouts: 0.24 us -> 3.78 us  [correlate(): return jnp.stack(pieces).reshape(7, 7, -1)]
    unnamed x194 -> x168, local copies, waits for them, and re-layouts: 5.57 us -> 5.21 us
  transfers between devices with their start and end apart: 13 -> 14, of which waited for: 6 -> 7; matrix products, arithmetic and copies ran while one was open for 19% -> 13% of each run, Pallas kernels for 0% -> 0%
where the time goes in v1:
time: 270 us; the launch traced here: 269 us
  waiting for transfers between devices  129 us (48%)
  starting transfers between devices  34.7 us (13%)
  other arithmetic  25.4 us (9%)
  local copies, waits for them, and re-layouts  25.2 us (9%)
  blocking collectives  20 us (7%)
  matrix products  19.3 us (7%)
  between operations  15.3 us (6%)
    psum x1, waiting for transfers between devices, on_device(): lax.psum(sample, link_axis)  56.9 us
    psum x1, waiting for transfers between devices, on_device(): lax.psum(lax.psum(sample, link_axis), axis_name=axis_key)  48.8 us
    psum x1, blocking collectives, on_device(): lax.psum(sample, link_axis)  13.2 us
    reduce_sum x1, other arithmetic, on_device(): inverse = lax.rsqrt(jnp.mean(update * update, -1, keepdims=True) + EPSILON)  10.5 us
    ppermute x4, starting transfers between devices, with_halo(): before = lax.ppermute(last, axis, up)  8.72 us
    all_to_all x1, waiting for transfers between devices, on_device(): lax.all_to_all(projected.reshape(batch_count, lat_rows, lon_cols, 3 * att...  8.46 us
    ppermute x4, starting transfers between devices, with_halo(): after = lax.ppermute(first, axis, down)  7.94 us
    psum x1, blocking collectives, on_device(): lax.psum(lax.psum(sample, link_axis), axis_name=axis_key)  6.79 us
  transfers between devices with their start and end apart: 14, of which 7 were waited for; matrix products, arithmetic and copies ran while one was open for 13% of the time, Pallas kernels for 0%

profile of v1, /device:TPU:0, one launch (start us, length us, event | category | flops | bytes accessed | tf_op | source)
XLA Modules:
  0.0 268.8 jit_solution(4022623047159432627)
XLA Ops:
  7.2 1.2 fusion.160
  8.4 3.1 %collective-permute-start = (bf16[1,32,3,512]{3,2,1,0:T(4,128)(2,1)S(1)}, bf16[1,32,3,512]{3,2,1,0:T(4,128)(2,1)S(1)}, u32[]{:S(2)}, u32[]{:S(2)}) collective-permute-start(bf16[1,32,3,512]{3,2,1,0:T(4,128)(2,1)S(1)} %get-tuple-element.96), channel_id=1, source_target_pairs={{0,4},{4,8},{8,12},{12,0},{1,5},{5,9},{9,13},{13,1},{2,6},{6,10},{... | collective-permute-start | bytes 294920 | tf_op jit(solution)/shard_map/ppermute | solution.py:18
  11.6 2.1 collective-permute-start.1
  13.6 1.9 fusion.15
  15.6 3.9 %all-to-all-start.2 = ((bf16[1,32,8,256]{3,2,0,1:T(8,128)(2,1)}), bf16[1,32,8,256]{3,2,0,1:T(8,128)(2,1)}, u32[]{:S(2)}, u32[]{:S(2)}) async-start(bf16[1,32,8,256]{3,2,0,1:T(8,128)(2,1)} %fusion.15), calls=%async_computation.2 | async-start | bytes 262144 | tf_op jit(solution)/shard_map/all_to_all | solution.py:140
  19.6 0.6 fusion.161
  20.3 0.7 fusion.162
  21.0 1.2 fusion.156
  22.2 3.5 %collective-permute-start.2 = (bf16[1,3,14,512]{3,2,1,0:T(8,128)(2,1)S(1)}, bf16[1,3,14,512]{3,2,1,0:T(8,128)(2,1)S(1)}, u32[]{:S(2)}, u32[]{:S(2)}) collective-permute-start(bf16[1,3,14,512]{3,2,1,0:T(8,128)(2,1)S(1)} %get-tuple-element.87), channel_id=1, source_target_pairs={{0,2},{1,3},{4,6},{5,7},{8,10},{9,11},{12,14},{13,15},{16,18},{17,... | collective-permute-start | bytes 129032 | tf_op jit(solution)/shard_map/ppermute | solution.py:18
  25.8 1.3 collective-permute-start.3
  27.1 0.6 fusion.163
  27.7 4.0 %collective-permute-done.3 = bf16[1,3,14,512]{3,2,1,0:T(8,128)(2,1)S(1)} collective-permute-done((bf16[1,3,14,512]{3,2,1,0:T(8,128)(2,1)S(1)}, bf16[1,3,14,512]{3,2,1,0:T(8,128)(2,1)S(1)}, u32[]{:S(2)}, u32[]{:S(2)}) %collective-permute-start.3) | collective-permute-done | bytes 43040 | tf_op jit(solution)/shard_map/ppermute | solution.py:19
  31.8 0.3 maximum_maximum_fusion
  32.1 1.9 slice_convert_fusion.2
  34.1 10.5 %multiply_reduce_fusion.51 = (f32[32,8]{1,0:T(8,128)S(1)}, f32[1,32,8,512]{3,2,1,0:T(8,128)S(1)}) fusion(f32[1,32,14,512]{3,2,1,0:T(8,128)S(1)} %get-tuple-element.80, f32[512]{0:T(512)} %bitcast.283, f32[512]{0:T(512)} %bitcast.285, f32[512]{0:T(512)S(1)} %bitcast.191, f32[512]{0:T(512)S(1)} %bitcast.193, f32[512]{0:T(512)S(1)} %bitcast.195, ...), kind=kLoop, calls=%fused_computation.293 | loop fusion | flops 13238016 | bytes 26577920 | tf_op jit(solution)/shard_map/reduce_sum | solution.py:119
  44.7 1.2 fusion.10
  45.8 5.0 %all-to-all-start = ((bf16[1,32,8,768]{3,2,0,1:T(8,128)(2,1)}), bf16[1,32,8,768]{3,2,0,1:T(8,128)(2,1)S(1)}, u32[]{:S(2)}, u32[]{:S(2)}) async-start(bf16[1,32,8,768]{3,2,0,1:T(8,128)(2,1)} %fusion.10), calls=%async_computation | async-start | bytes 786432 | tf_op jit(solution)/shard_map/all_to_all | solution.py:123
  50.9 0.9 copy.83
  51.9 8.5 %all-to-all-done = bf16[1,32,8,768]{3,2,0,1:T(8,128)(2,1)S(1)} async-done(((bf16[1,32,8,768]{3,2,0,1:T(8,128)(2,1)}), bf16[1,32,8,768]{3,2,0,1:T(8,128)(2,1)S(1)}, u32[]{:S(2)}, u32[]{:S(2)}) %all-to-all-start) | async-done | bytes 393248 | tf_op jit(solution)/shard_map/all_to_all | solution.py:123
  60.7 0.9 reshape.609
  61.7 2.1 fusion.164
  63.8 1.1 fusion.129
  64.8 2.0 fusion.14
  66.8 1.8 fusion.11
  68.6 2.3 fusion.12
  70.9 1.1 copy.88
  72.0 0.2 convert_element_type.322
  72.2 1.1 copy.99
  73.3 0.9 reshape.619
  74.2 3.9 %all-to-all-start.1 = ((bf16[1,8,32,256]{3,1,0,2:T(8,128)(2,1)}), bf16[1,8,32,256]{3,1,0,2:T(8,128)(2,1)}, u32[]{:S(2)}, u32[]{:S(2)}) async-start(bf16[1,8,32,256]{3,1,0,2:T(8,128)(2,1)} %reshape.619), calls=%async_computation.1 | async-start | bytes 262144 | tf_op jit(solution)/shard_map/all_to_all | solution.py:131
  78.2 2.3 fusion.13
  80.5 1.1 copy.90
  81.8 1.1 copy.92
  83.1 1.0 copy.93
  84.1 5.1 %all-to-all-start.3 = ((bf16[1,8,32,768]{3,1,0,2:T(8,128)(2,1)}), bf16[1,8,32,768]{3,1,0,2:T(8,128)(2,1)}, u32[]{:S(2)}, u32[]{:S(2)}) async-start(bf16[1,8,32,768]{3,1,0,2:T(8,128)(2,1)} %copy.93), calls=%async_computation.3 | async-start | bytes 786432 | tf_op jit(solution)/shard_map/all_to_all | solution.py:148
  89.3 1.0 constant_dynamic-update-slice_fusion
  90.3 1.1 copy.134
  91.4 0.6 copy-done.9
  92.1 1.0 fusion.122
  93.1 5.1 %all-to-all-done.3 = bf16[1,8,32,768]{3,1,0,2:T(8,128)(2,1)} async-done(((bf16[1,8,32,768]{3,1,0,2:T(8,128)(2,1)}), bf16[1,8,32,768]{3,1,0,2:T(8,128)(2,1)}, u32[]{:S(2)}, u32[]{:S(2)}) %all-to-all-start.3) | async-done | bytes 393248 | tf_op jit(solution)/shard_map/all_to_all | solution.py:148
  98.3 1.1 copy.132
  99.4 1.0 multiply_reduce_fusion.1
  100.4 1.6 fusion.139
  102.0 2.3 multiply_reduce_fusion.2
  104.3 2.0 multiply_reduce_fusion.29
  106.4 1.7 multiply_reduce_fusion.20
  108.1 3.8 %stack.199 = f32[49,512]{1,0:T(8,128)S(1)} concatenate(f32[1,512]{1,0:T(1,128)} %bitcast.333, f32[1,512]{1,0:T(1,128)} %bitcast.334, f32[1,512]{1,0:T(1,128)} %bitcast.335, f32[1,512]{1,0:T(1,128)} %bitcast.322, f32[1,512]{1,0:T(1,128)} %bitcast.321, f32[1,512]{1,0:T(1,128)} %bitcast.320, f32[1,512]{1,0:T(1,128)} %bitcast.319, f32[1,512]{1,0:T(1,128)} %bitcast.318, ...), dimensions={0} | concatenate | bytes 200704 | tf_op jit(solution)/shard_map/stack | solution.py:46
  111.9 0.7 reshape.617
  112.8 0.6 collective-permute-start.4
  113.4 3.3 %collective-permute-start.5 = (bf16[1,32,3,512]{3,2,1,0:T(4,128)(2,1)S(1)}, bf16[1,32,3,512]{3,2,1,0:T(4,128)(2,1)S(1)}, u32[]{:S(2)}, u32[]{:S(2)}) collective-permute-start(bf16[1,32,3,512]{3,2,1,0:T(4,128)(2,1)S(1)} %get-tuple-element.95), channel_id=1, source_target_pairs={{4,0},{8,4},{12,8},{0,12},{5,1},{9,5},{13,9},{1,13},{6,2},{10,6},{... | collective-permute-start | bytes 294920 | tf_op jit(solution)/shard_map/ppermute | solution.py:19
  116.6 3.1 %collective-permute-done.4 = bf16[1,32,3,512]{3,2,1,0:T(4,128)(2,1)S(1)} collective-permute-done((bf16[1,32,3,512]{3,2,1,0:T(4,128)(2,1)S(1)}, bf16[1,32,3,512]{3,2,1,0:T(4,128)(2,1)S(1)}, u32[]{:S(2)}, u32[]{:S(2)}) %collective-permute-start.4) | collective-permute-done | bytes 98336 | tf_op jit(solution)/shard_map/ppermute | solution.py:18
  119.7 2.3 collective-permute-done.5
  122.1 1.5 collective-permute-start.6
  123.5 1.3 collective-permute-start.7
  124.8 0.9 fusion.9
  125.8 13.2 %psum.62 = f32[512]{0:T(512)S(1)} all-reduce(f32[512]{0:T(512)S(1)} %copy-done.78), channel_id=1, replica_groups=mesh['member'=2,'lon'=4,'lat'=2,'dp'=2] {'lon'}, use_global_device_ids=true, to_apply=%region_61.0 | all-reduce | flops 512 | bytes 4096 | tf_op jit(solution)/shard_map/psum | solution.py:172
  139.0 6.8 %psum.63 = f32[512]{0:T(512)} all-reduce(f32[512]{0:T(512)S(1)} %psum.62), channel_id=1, replica_groups=mesh['member'=2,'lon'=4,'lat'=2,'dp'=2] {'lat','dp'}, use_global_device_ids=true, to_apply=%region_62.0 | all-reduce | flops 512 | bytes 4096 | tf_op jit(solution)/shard_map/psum | solution.py:171
  145.8 56.9 %all-reduce.7.cloned.1.call-done = (f32[512,768]{1,0:T(8,128)}, f32[256,512]{1,0:T(8,128)}, f32[7,7,512]{2,1,0:T(8,128)}) async-done(((f32[512,768]{1,0:T(8,128)}, f32[256,512]{1,0:T(8,128)}, f32[7,7,512]{2,1,0:T(8,128)}), (f32[512,768]{1,0:T(8,128)}, f32[256,512]{1,0:T(8,128)}, f32[7,7,512]{2,1,0:T(8,128)})) %all-reduce.7.cloned.1.call-update) | async-done | bytes 2197520 | tf_op jit(solution)/shard_map/psum | solution.py:172
  203.2 0.3 maximum_convert_fusion
  203.8 5.2 %fusion.24 = bf16[1,32,8,512]{3,2,1,0:T(8,128)(2,1)} fusion(f32[1,32,8,512]{3,2,1,0:T(8,128)S(1)} %get-tuple-element.73, f32[1,38,14,512]{3,2,1,0:T(8,128)S(1)} %maximum_convert_fusion, f32[512]{0:T(512)} %bitcast.284, f32[512]{0:T(512)} %bitcast.286, f32[512]{0:T(512)S(1)} %bitcast.192, f32[512]{0:T(512)S(1)} %bitcast.194, f32[512]{0:T(512)S(1)} %bitcast.196, ...), kind=kLoop, calls=%fused_computation.42 | loop fusion | flops 12976128 | bytes 26576896 | tf_op jit(solution)/shard_map/convert_element_type | solution.py:169
  209.0 48.8 %all-reduce.5.cloned.1.call-done = (f32[512,768]{1,0:T(8,128)}, f32[256,512]{1,0:T(8,128)}, f32[7,7,512]{2,1,0:T(8,128)}) async-done(((f32[512,768]{1,0:T(8,128)}, f32[256,512]{1,0:T(8,128)}, f32[7,7,512]{2,1,0:T(8,128)}), (f32[512,768]{1,0:T(8,128)}, f32[256,512]{1,0:T(8,128)}, f32[7,7,512]{2,1,0:T(8,128)})) %all-reduce.5.cloned.1.call-update) | async-done | bytes 2197520 | tf_op jit(solution)/shard_map/psum | solution.py:171
  257.8 2.7 %copy.142 = f32[512,768]{1,0:T(8,128)} copy(f32[512,768]{1,0:T(8,128)} %get-tuple-element.157) | data formatting | bytes 3145728
  260.5 0.8 copy.143
  261.3 0.6 copy.144
  (190 shorter events, 1.7 us)
Async XLA Ops:
  7.2 37.5 %copy-start = (bf16[512,768]{1,0:T(8,128)(2,1)S(1)}, bf16[512,768]{1,0:T(8,128)(2,1)}, u32[]{:S(2)}) copy-start(bf16[512,768]{1,0:T(8,128)(2,1)} %param.10) | copy-start | bytes 2359300
  7.2 13.8 %copy-start.1 = (bf16[1,32,8,512]{3,2,1,0:T(8,128)(2,1)S(1)}, bf16[1,32,8,512]{3,2,1,0:T(8,128)(2,1)}, u32[]{:S(2)}) copy-start(bf16[1,32,8,512]{3,2,1,0:T(8,128)(2,1)} %param.6) | copy-start | bytes 786436
  7.2 12.3 %copy-start.17 = (f32[7,7,512]{2,1,0:T(8,128)S(1)}, f32[7,7,512]{2,1,0:T(8,128)}, u32[]{:S(2)}) copy-start(f32[7,7,512]{2,1,0:T(8,128)} %param.8) | copy-start | bytes 301060
  8.4 12.5 %collective-permute-start = (bf16[1,32,3,512]{3,2,1,0:T(4,128)(2,1)S(1)}, bf16[1,32,3,512]{3,2,1,0:T(4,128)(2,1)S(1)}, u32[]{:S(2)}, u32[]{:S(2)}) collective-permute-start(bf16[1,32,3,512]{3,2,1,0:T(4,128)(2,1)S(1)} %get-tuple-element.96), channel_id=1, source_target_pairs={{0,4},{4,8},{8,12},{12,0},{1,5},{5,9},{9,13},{13,1},{2,6},{6,10},{... | collective-permute-start | bytes 294920 | tf_op jit(solution)/shard_map/ppermute | solution.py:18
  11.6 9.4 %collective-permute-start.1 = (bf16[1,32,3,512]{3,2,1,0:T(4,128)(2,1)S(1)}, bf16[1,32,3,512]{3,2,1,0:T(4,128)(2,1)S(1)}, u32[]{:S(2)}, u32[]{:S(2)}) collective-permute-start(bf16[1,32,3,512]{3,2,1,0:T(4,128)(2,1)S(1)} %get-tuple-element.97), channel_id=1, source_target_pairs={{4,0},{8,4},{12,8},{0,12},{5,1},{9,5},{13,9},{1,13},{6,2},{10,6},{... | collective-permute-start | bytes 294920 | tf_op jit(solution)/shard_map/ppermute | solution.py:19
  15.6 30.2 %all-to-all-start.2 = ((bf16[1,32,8,256]{3,2,0,1:T(8,128)(2,1)}), bf16[1,32,8,256]{3,2,0,1:T(8,128)(2,1)}, u32[]{:S(2)}, u32[]{:S(2)}) async-start(bf16[1,32,8,256]{3,2,0,1:T(8,128)(2,1)} %fusion.15), calls=%async_computation.2 | async-start | bytes 262144 | tf_op jit(solution)/shard_map/all_to_all | solution.py:140
  20.2 13.8 %copy-start.19 = (f32[1,1,512]{2,1,0:T(1,128)}, f32[1,1,512]{2,1,0:T(1,128)S(1)}, u32[]{:S(2)}) copy-start(f32[1,1,512]{2,1,0:T(1,128)S(1)} %get-tuple-element.101) | copy-start | bytes 6148
  20.2 13.8 %copy-start.21 = (f32[1,1,512]{2,1,0:T(1,128)}, f32[1,1,512]{2,1,0:T(1,128)S(1)}, u32[]{:S(2)}) copy-start(f32[1,1,512]{2,1,0:T(1,128)S(1)} %get-tuple-element.102) | copy-start | bytes 6148
  20.2 13.8 %copy-start.23 = (f32[1,1,512]{2,1,0:T(1,128)}, f32[1,1,512]{2,1,0:T(1,128)S(1)}, u32[]{:S(2)}) copy-start(f32[1,1,512]{2,1,0:T(1,128)S(1)} %get-tuple-element.103) | copy-start | bytes 6148
  20.2 13.8 %copy-start.25 = (f32[1,1,512]{2,1,0:T(1,128)}, f32[1,1,512]{2,1,0:T(1,128)S(1)}, u32[]{:S(2)}) copy-start(f32[1,1,512]{2,1,0:T(1,128)S(1)} %get-tuple-element.104) | copy-start | bytes 6148
  20.2 13.8 %copy-start.27 = (f32[1,1,512]{2,1,0:T(1,128)}, f32[1,1,512]{2,1,0:T(1,128)S(1)}, u32[]{:S(2)}) copy-start(f32[1,1,512]{2,1,0:T(1,128)S(1)} %get-tuple-element.105) | copy-start | bytes 6148
  20.2 13.8 %copy-start.29 = (f32[1,1,512]{2,1,0:T(1,128)}, f32[1,1,512]{2,1,0:T(1,128)S(1)}, u32[]{:S(2)}) copy-start(f32[1,1,512]{2,1,0:T(1,128)S(1)} %get-tuple-element.106) | copy-start | bytes 6148
  20.2 13.8 %copy-start.31 = (f32[1,1,512]{2,1,0:T(1,128)}, f32[1,1,512]{2,1,0:T(1,128)S(1)}, u32[]{:S(2)}) copy-start(f32[1,1,512]{2,1,0:T(1,128)S(1)} %get-tuple-element.107) | copy-start | bytes 6148
  20.2 13.8 %copy-start.33 = (f32[1,1,512]{2,1,0:T(1,128)}, f32[1,1,512]{2,1,0:T(1,128)S(1)}, u32[]{:S(2)}) copy-start(f32[1,1,512]{2,1,0:T(1,128)S(1)} %get-tuple-element.108) | copy-start | bytes 6148
  20.2 13.8 %copy-start.35 = (f32[1,1,512]{2,1,0:T(1,128)}, f32[1,1,512]{2,1,0:T(1,128)S(1)}, u32[]{:S(2)}) copy-start(f32[1,1,512]{2,1,0:T(1,128)S(1)} %get-tuple-element.109) | copy-start | bytes 6148
  20.2 13.8 %copy-start.37 = (f32[1,1,512]{2,1,0:T(1,128)}, f32[1,1,512]{2,1,0:T(1,128)S(1)}, u32[]{:S(2)}) copy-start(f32[1,1,512]{2,1,0:T(1,128)S(1)} %get-tuple-element.110) | copy-start | bytes 6148
  20.9 11.2 %copy-start.6 = (bf16[1,32,3,512]{3,2,1,0:T(4,128)(2,1)}, bf16[1,32,3,512]{3,2,1,0:T(4,128)(2,1)S(1)}, u32[]{:S(2)}) copy-start(bf16[1,32,3,512]{3,2,1,0:T(4,128)(2,1)S(1)} %collective-permute-done) | copy-start | bytes 294916
  21.0 11.1 %copy-start.8 = (bf16[1,32,3,512]{3,2,1,0:T(4,128)(2,1)}, bf16[1,32,3,512]{3,2,1,0:T(4,128)(2,1)S(1)}, u32[]{:S(2)}) copy-start(bf16[1,32,3,512]{3,2,1,0:T(4,128)(2,1)S(1)} %collective-permute-done.1) | copy-start | bytes 294916
  22.2 5.5 %collective-permute-start.2 = (bf16[1,3,14,512]{3,2,1,0:T(8,128)(2,1)S(1)}, bf16[1,3,14,512]{3,2,1,0:T(8,128)(2,1)S(1)}, u32[]{:S(2)}, u32[]{:S(2)}) collective-permute-start(bf16[1,3,14,512]{3,2,1,0:T(8,128)(2,1)S(1)} %get-tuple-element.87), channel_id=1, source_target_pairs={{0,2},{1,3},{4,6},{5,7},{8,10},{9,11},{12,14},{13,15},{16,18},{17,... | collective-permute-start | bytes 129032 | tf_op jit(solution)/shard_map/ppermute | solution.py:18
  25.8 6.0 %collective-permute-start.3 = (bf16[1,3,14,512]{3,2,1,0:T(8,128)(2,1)S(1)}, bf16[1,3,14,512]{3,2,1,0:T(8,128)(2,1)S(1)}, u32[]{:S(2)}, u32[]{:S(2)}) collective-permute-start(bf16[1,3,14,512]{3,2,1,0:T(8,128)(2,1)S(1)} %get-tuple-element.88), channel_id=1, source_target_pairs={{2,0},{3,1},{6,4},{7,5},{10,8},{11,9},{14,12},{15,13},{18,16},{19,... | collective-permute-start | bytes 129032 | tf_op jit(solution)/shard_map/ppermute | solution.py:19
  34.1 10.6 %copy-start.18 = (f32[512]{0:T(512)S(1)}, f32[512]{0:T(512)}, u32[]{:S(2)}) copy-start(f32[512]{0:T(512)} %param.9) | copy-start | bytes 6148
  45.8 14.6 %all-to-all-start = ((bf16[1,32,8,768]{3,2,0,1:T(8,128)(2,1)}), bf16[1,32,8,768]{3,2,0,1:T(8,128)(2,1)S(1)}, u32[]{:S(2)}, u32[]{:S(2)}) async-start(bf16[1,32,8,768]{3,2,0,1:T(8,128)(2,1)} %fusion.10), calls=%async_computation | async-start | bytes 786432 | tf_op jit(solution)/shard_map/all_to_all | solution.py:123
  60.6 4.2 %copy-start.14 = (bf16[8,32,4,64]{3,2,1,0:T(4,128)(2,1)}, bf16[8,32,4,64]{3,2,1,0:T(4,128)(2,1)S(1)}, u32[]{:S(2)}) copy-start(bf16[8,32,4,64]{3,2,1,0:T(4,128)(2,1)S(1)} %reshape.608) | copy-start | bytes 393220
  63.8 1.1 copy-start.80
  64.8 2.0 copy-start.79
  66.8 1.8 copy-start.13
  66.8 1.8 copy-start.15
  70.9 7.2 %copy-start.81 = (f32[8,4,32]{2,1,0:T(4,128)S(1)}, f32[8,4,32]{2,1,0:T(4,128)}, u32[]{:S(2)}) copy-start(f32[8,4,32]{2,1,0:T(4,128)} %copy-done.80) | copy-start | bytes 12292
  74.2 9.9 %all-to-all-start.1 = ((bf16[1,8,32,256]{3,1,0,2:T(8,128)(2,1)}), bf16[1,8,32,256]{3,1,0,2:T(8,128)(2,1)}, u32[]{:S(2)}, u32[]{:S(2)}) async-start(bf16[1,8,32,256]{3,1,0,2:T(8,128)(2,1)} %reshape.619), calls=%async_computation.1 | async-start | bytes 262144 | tf_op jit(solution)/shard_map/all_to_all | solution.py:131
  83.1 6.2 %copy-start.2 = (bf16[1,32,8,512]{3,2,1,0:T(8,128)(2,1)S(1)}, bf16[1,32,8,512]{3,2,1,0:T(8,128)(2,1)}, u32[]{:S(2)}) copy-start(bf16[1,32,8,512]{3,2,1,0:T(8,128)(2,1)} %param.6) | copy-start | bytes 786436
  84.1 8.0 %copy-start.3 = (bf16[1,32,8,512]{3,2,1,0:T(8,128)(2,1)S(1)}, bf16[1,32,8,512]{3,2,1,0:T(8,128)(2,1)}, u32[]{:S(2)}) copy-start(bf16[1,32,8,512]{3,2,1,0:T(8,128)(2,1)} %param.7) | copy-start | bytes 786436
  84.1 14.1 %all-to-all-start.3 = ((bf16[1,8,32,768]{3,1,0,2:T(8,128)(2,1)}), bf16[1,8,32,768]{3,1,0,2:T(8,128)(2,1)}, u32[]{:S(2)}, u32[]{:S(2)}) async-start(bf16[1,8,32,768]{3,1,0,2:T(8,128)(2,1)} %copy.93), calls=%async_computation.3 | async-start | bytes 786432 | tf_op jit(solution)/shard_map/all_to_all | solution.py:148
  89.3 113.5 %all-reduce.7.cloned.1.call-start = ((), (), s32[]{:S(2)}) async-start(), calls=%async_computation.5 | async-start | bytes 4423680 | tf_op jit(solution)/shard_map/psum | solution.py:172
  90.3 9.0 %copy-start.4 = (bf16[1,32,11,512]{3,2,1,0:T(8,128)(2,1)}, bf16[1,32,11,512]{3,2,1,0:T(8,128)(2,1)S(1)}, u32[]{:S(2)}) copy-start(bf16[1,32,11,512]{3,2,1,0:T(8,128)(2,1)S(1)} %constant_dynamic-update-slice_fusion) | copy-start | bytes 1081348
  104.3 2.0 copy-start.5
  104.3 2.0 copy-start.7
  106.3 1.8 copy-start.69
  106.3 1.8 copy-start.70
  106.3 1.8 copy-start.71
  106.3 1.8 copy-start.72
  106.3 1.8 copy-start.73
  106.3 1.8 copy-start.74
  106.3 1.8 copy-start.75
  106.4 1.8 copy-start.76
  106.4 1.8 copy-start.77
  112.6 12.2 %copy-start.10 = (bf16[1,4,8,8,256]{4,3,2,1,0:T(8,128)(2,1)S(1)}, bf16[1,4,8,8,256]{4,3,2,1,0:T(8,128)(2,1)}, u32[]{:S(2)}) copy-start(bf16[1,4,8,8,256]{4,3,2,1,0:T(8,128)(2,1)} %copy-done.9) | copy-start | bytes 393220
  112.6 12.3 %copy-start.11 = (bf16[256,512]{1,0:T(8,128)(2,1)S(1)}, bf16[256,512]{1,0:T(8,128)(2,1)}, u32[]{:S(2)}) copy-start(bf16[256,512]{1,0:T(8,128)(2,1)} %param.11) | copy-start | bytes 786436
  112.6 13.2 %copy-start.78 = (f32[512]{0:T(512)S(1)}, f32[512]{0:T(512)}, u32[]{:S(2)}) copy-start(f32[512]{0:T(512)} %get-tuple-element.48) | copy-start | bytes 6148
  112.6 145.2 %all-reduce.5.cloned.1.call-start = ((), (), s32[]{:S(2)}) async-start(), calls=%async_computation.4 | async-start | bytes 4423680 | tf_op jit(solution)/shard_map/psum | solution.py:171
  112.8 7.0 %collective-permute-start.4 = (bf16[1,32,3,512]{3,2,1,0:T(4,128)(2,1)S(1)}, bf16[1,32,3,512]{3,2,1,0:T(4,128)(2,1)S(1)}, u32[]{:S(2)}, u32[]{:S(2)}) collective-permute-start(bf16[1,32,3,512]{3,2,1,0:T(4,128)(2,1)S(1)} %get-tuple-element.94), channel_id=1, source_target_pairs={{0,4},{4,8},{8,12},{12,0},{1,5},{5,9},{9,13},{13,1},{2,6},{6,10},{... | collective-permute-start | bytes 294920 | tf_op jit(solution)/shard_map/ppermute | solution.py:18
  113.4 8.6 %collective-permute-start.5 = (bf16[1,32,3,512]{3,2,1,0:T(4,128)(2,1)S(1)}, bf16[1,32,3,512]{3,2,1,0:T(4,128)(2,1)S(1)}, u32[]{:S(2)}, u32[]{:S(2)}) collective-permute-start(bf16[1,32,3,512]{3,2,1,0:T(4,128)(2,1)S(1)} %get-tuple-element.95), channel_id=1, source_target_pairs={{4,0},{8,4},{12,8},{0,12},{5,1},{9,5},{13,9},{1,13},{6,2},{10,6},{... | collective-permute-start | bytes 294920 | tf_op jit(solution)/shard_map/ppermute | solution.py:19
  122.1 81.1 %collective-permute-start.6 = (bf16[1,3,14,512]{3,2,1,0:T(8,128)(2,1)S(1)}, bf16[1,3,14,512]{3,2,1,0:T(8,128)(2,1)S(1)}, u32[]{:S(2)}, u32[]{:S(2)}) collective-permute-start(bf16[1,3,14,512]{3,2,1,0:T(8,128)(2,1)S(1)} %get-tuple-element.83), channel_id=1, source_target_pairs={{0,2},{1,3},{4,6},{5,7},{8,10},{9,11},{12,14},{13,15},{16,18},{17,... | collective-permute-start | bytes 129032 | tf_op jit(solution)/shard_map/ppermute | solution.py:18
  123.5 79.7 %collective-permute-start.7 = (bf16[1,3,14,512]{3,2,1,0:T(8,128)(2,1)S(1)}, bf16[1,3,14,512]{3,2,1,0:T(8,128)(2,1)S(1)}, u32[]{:S(2)}, u32[]{:S(2)}) collective-permute-start(bf16[1,3,14,512]{3,2,1,0:T(8,128)(2,1)S(1)} %get-tuple-element.84), channel_id=1, source_target_pairs={{2,0},{3,1},{6,4},{7,5},{10,8},{11,9},{14,12},{15,13},{18,16},{19,... | collective-permute-start | bytes 129032 | tf_op jit(solution)/shard_map/ppermute | solution.py:19
  202.8 0.7 copy-start.20
  202.9 0.7 copy-start.39
  202.9 0.7 copy-start.42
  203.0 0.7 copy-start.48
  203.0 0.7 copy-start.49
  203.0 0.7 copy-start.55
  203.0 0.7 copy-start.56
  203.1 0.7 copy-start.65
  203.1 0.7 copy-start.66
  257.8 2.7 %copy-start.12 = (f32[256,512]{1,0:T(8,128)S(1)}, f32[256,512]{1,0:T(8,128)}, u32[]{:S(2)}) copy-start(f32[256,512]{1,0:T(8,128)} %get-tuple-element.158) | copy-start | bytes 1572868
  257.8 3.5 %copy-start.16 = (f32[7,7,512]{2,1,0:T(8,128)S(1)}, f32[7,7,512]{2,1,0:T(8,128)}, u32[]{:S(2)}) copy-start(f32[7,7,512]{2,1,0:T(8,128)} %get-tuple-element.159) | copy-start | bytes 301060
  (32 other events, 21.8 us)
Sparse Core Ops, SparseCore 0:
  112.7 89.9 all-reduce.6
  205.3 52.4 all-reduce.4
